TPU v7x, 32 devices: a whole 2x2x4 slice. The times are simulated.
32 devices in a mesh: term: 2 (over x), sector: 16 (over z, y, core).
Axes of the slice: x: 2, y: 2, z: 4, core: 2. Of those that a mesh axis runs over, the one named last changes fastest.
Arguments:
- psi_start: bfloat16 [128, 256, 256], P('sector'), may hold values from -6 to 6
- left_env: bfloat16 [6, 128, 256, 256], P('term', 'sector')
- right_env: bfloat16 [6, 128, 256, 256], P('term', 'sector')
- connect: int32 [6, 128], P('term', 'sector'), may hold values from 0 to 127, as said below
- sector_dims: int32 [2, 128], P(None, 'sector'), may hold values from 64 to 256
- precond: bfloat16 [128, 256, 256], P('sector'), may hold values from 0.5 to 4
Outputs:
- projected: float32 [3, 3], replicated
- last_vector: float32 [128, 256, 256], P('sector', 'term')
- new_env: bfloat16 [6, 128, 256, 256], P('term', 'sector')
Inputs may be any that keep to these rules, and one draw needn't show every extreme that they name: connect[t, s] differs from s by at most 8.
All inputs are finite; a program needn't handle non-finite values.
Results may differ from a plain program's by a relative error of at most 0.012.
Values may be sent and summed in bfloat16 or wider, within the bound.
A program may use at most 128 MiB of HBM per device.

v0:
```python
import functools
import jax
import jax.numpy as jnp
from jax import lax
from jax.experimental import pallas as pl
from jax.experimental.pallas import tpu as pltpu
from jax.sharding import PartitionSpec as P

epsilon = 1e-06
MESH = pl.DeviceIdType.MESH
F32 = jnp.float32
BF16 = jnp.bfloat16


def fold(values):
    rows, width = values.shape
    total = values.reshape(rows // 8, 8, width).sum(axis=0)
    out = total[:, :128]
    for start in range(128, width, 128):
        out = out + total[:, start : start + 128]
    return out


def kernel(
    sizes,
    dims, conn, psi_in, left_in, right_in, pre_in,
    proj, last_out, env_out,
    left, right, pre, env, psi, last, inverse_of, raw, ext1, ext2, ext3, acc, stage, came, sig1, sig2, base1, base2, tile, slots,
    halo_send, halo_recv, relay_send, share_send, share_recv, part_send, part_recv, sum_send, sum_recv, load, store,
):
    pieces, devices, terms, blocks, width, entries = sizes
    share = width // pieces
    count = pieces * devices
    step = min(32, share)
    steps = share // step
    me_t = lax.axis_index("term")
    me_s = lax.axis_index("sector")
    me = me_t * devices + me_s
    first = me_s * blocks - blocks
    has_low = me_s > 0
    has_high = me_s < devices - 1
    odd = lax.rem(me_s, 2) == 1
    even = jnp.logical_not(odd)
    zero = jnp.zeros((8, 128), F32)

    def device_at(offset):
        other = lax.rem(me + offset, count)
        return (other // devices, lax.rem(other, devices))

    def term_at(offset):
        return lax.rem(me_t + offset, pieces)

    def rows_of(piece):
        return pl.ds(pl.multiple_of(piece * share, share), share)

    half = blocks // 2
    loads = [
        pltpu.make_async_copy(source, target, load.at[i])
        for i, (source, target) in enumerate(
            ((psi_in, psi), (pre_in, pre), (left_in, left), (right_in, right))
        )
    ]
    for one in loads:
        one.start()
    barrier = pltpu.get_barrier_semaphore()

    @pl.loop(1, count)
    def _(offset):
        pl.semaphore_signal(barrier, inc=1, device_id=device_at(offset), device_id_type=MESH)

    def halo_copy(ref, s, j, up, rows):
        slot = s if up else 2 * blocks + s
        direction = 0 if up else 1
        return pltpu.make_async_remote_copy(
            src_ref=ref.at[blocks + s, rows],
            dst_ref=ref.at[slot, rows],
            send_sem=halo_send.at[direction, j, s],
            recv_sem=halo_recv.at[direction, j, s],
            device_id=(me_t, me_s + 1 if up else me_s - 1),
            device_id_type=MESH,
        )

    def sends(j, s, relayed):
        if j == 0:
            return has_high, has_low
        far = s < relayed
        return (
            has_high & jnp.logical_not(odd & far),
            has_low & jnp.logical_not(even & far),
        )

    def halo_start(ref, s, j, relayed):
        rows = rows_of(term_at(pieces - j))
        up, down = sends(j, s, relayed)

        @pl.when(up)
        def _():
            halo_copy(ref, s, j, True, rows).start()

        @pl.when(down)
        def _():
            halo_copy(ref, s, j, False, rows).start()

    def relay_copy(ref, s, j, up):
        slot = s if up else 2 * blocks + s
        return pltpu.make_async_remote_copy(
            src_ref=ref.at[slot, rows_of(me_t)],
            dst_ref=ref.at[slot, rows_of(me_t)],
            send_sem=relay_send.at[j - 1, s],
            recv_sem=halo_recv.at[0 if up else 1, j, s],
            device_id=(term_at(j), me_s),
            device_id_type=MESH,
        )

    def relay(ref, s, relayed):
        for up, here in ((True, has_low & even), (False, has_high & odd)):

            @pl.when(here & (s < relayed))
            def _():
                halo_copy(ref, s, 0, up, rows_of(me_t)).wait_recv()
                for j in range(1, pieces):
                    relay_copy(ref, s, j, up).start()

    def halo_wait(ref, s, relayed):
        far = s < relayed
        for j in range(pieces):
            rows = rows_of(term_at(pieces - j))
            up, down = sends(j, s, relayed)

            @pl.when(up)
            def _():
                halo_copy(ref, s, j, True, rows).wait_send()

            @pl.when(down)
            def _():
                halo_copy(ref, s, j, False, rows).wait_send()

            low, high = has_low, has_high
            if j == 0:
                low = low & jnp.logical_not(even & far)
                high = high & jnp.logical_not(odd & far)

            @pl.when(low)
            def _():
                halo_copy(ref, s, j, True, rows).wait_recv()

            @pl.when(high)
            def _():
                halo_copy(ref, s, j, False, rows).wait_recv()

        for up, here in ((True, has_low & even), (False, has_high & odd)):

            @pl.when(here & far)
            def _():
                for j in range(1, pieces):
                    relay_copy(ref, s, j, up).wait_send()

    def share_copy(ref, s, offset, piece):
        return pltpu.make_async_remote_copy(
            src_ref=ref.at[blocks + s, rows_of(piece)],
            dst_ref=ref.at[blocks + s, rows_of(piece)],
            send_sem=share_send.at[offset - 1, s],
            recv_sem=share_recv.at[offset - 1, s],
            device_id=(term_at(offset), me_s),
            device_id_type=MESH,
        )

    def part_copy(s, offset):
        return pltpu.make_async_remote_copy(
            src_ref=stage.at[offset - 1, s],
            dst_ref=came.at[offset - 1, s],
            send_sem=part_send.at[offset - 1, s],
            recv_sem=part_recv.at[offset - 1, s],
            device_id=(term_at(offset), me_s),
            device_id_type=MESH,
        )

    lane = lax.broadcasted_iota(jnp.int32, (1, 128), 1)

    def sum_start(which, tiles):
        packed = jnp.zeros((1, 128), F32)
        for i, one in enumerate(tiles):
            row = jnp.sum(one, axis=0, keepdims=True)
            packed = jnp.where(lane == i, jnp.sum(row, axis=1, keepdims=True), packed)
        tile[which] = packed
        slots[which, me] = packed

        @pl.loop(1, count)
        def _(offset):
            pltpu.make_async_remote_copy(
                src_ref=tile.at[which],
                dst_ref=slots.at[which, me],
                send_sem=sum_send.at[which],
                recv_sem=sum_recv.at[which],
                device_id=device_at(offset),
                device_id_type=MESH,
            ).start()

    def sum_finish(which):
        others = slots.at[which, pl.ds(0, count - 1)]
        pltpu.make_async_copy(others, others, sum_recv.at[which]).wait()
        full = jnp.sum(slots[which], axis=0) / entries
        return lambda i: full[:, i : i + 1]

    row_ids = lax.broadcasted_iota(jnp.int32, (width, width), 0)
    col_ids = lax.broadcasted_iota(jnp.int32, (width, width), 1)

    loads[0].wait()

    @pl.loop(0, blocks)
    def _(s):
        keep = (row_ids < dims[0, s]) & (col_ids < dims[1, s])
        raw[blocks + s] = jnp.where(keep, psi[s].astype(F32), 0.0).astype(BF16)

    pl.semaphore_wait(barrier, count - 1)

    @pl.loop(0, blocks)
    def _(s):
        for j in range(pieces):
            halo_start(raw, s, j, blocks)

    starts = [k * step for k in range(steps)]

    def own_rows(start):
        return pl.ds(pl.multiple_of(me_t * share + start, step), step)

    def norm_step(s, total):
        for start in starts:
            v = raw[blocks + s, own_rows(start), :].astype(F32)
            total = total + fold(v * v)
        return total

    sum_start(0, [lax.fori_loop(0, blocks, norm_step, zero)])
    loads[1].wait()

    @pl.loop(0, blocks)
    def _(s):
        for start in starts:
            inverse_of[s, pl.ds(start, step), :] = 1.0 / pre[s, own_rows(start), :].astype(F32)

    @pl.loop(0, blocks)
    def _(s):
        relay(raw, s, blocks)

    norm = sum_finish(0)(0)
    scale = 1.0 / jnp.sqrt(norm + epsilon)

    def scaled(slot):
        ext1[slot] = (raw[slot].astype(F32) * scale).astype(BF16)

    @pl.loop(0, blocks)
    def _(s):
        scaled(blocks + s)
        base1[s] = raw[blocks + s, rows_of(me_t), :].astype(F32) * scale

    @pl.loop(0, blocks)
    def _(s):
        halo_wait(raw, s, blocks)

        @pl.when(has_low)
        def _():
            scaled(s)

        @pl.when(has_high)
        def _():
            scaled(2 * blocks + s)

    def product(ref, s, keep):
        halves = []
        for t in range(terms):
            source = ref[jnp.clip(conn[t, s] - first, 0, 3 * blocks - 1)]
            one = jnp.dot(left[t, s], source, preferred_element_type=F32).astype(BF16)
            halves.append(one)
            if keep:
                env[t, s] = one
        total = None
        for t in range(terms):
            one = lax.dot_general(
                halves[t], right[t, s], (((1,), (1,)), ((), ())), preferred_element_type=F32
            )
            total = one if total is None else total + one
        return total

    def apply(ref):
        @pl.loop(0, blocks)
        def _(s):
            acc[s] = product(ref, s, False)
            for offset in range(1, pieces):
                stage[offset - 1, s] = acc[s, rows_of(term_at(offset)), :].astype(BF16)
                part_copy(s, offset).start()

    def masked_sum(s, start):
        total = acc[s, own_rows(start), :]
        for offset in range(1, pieces):
            total = total + came[offset - 1, s, pl.ds(start, step), :].astype(F32)
        rows = lax.broadcasted_iota(jnp.int32, (step, width), 0) + (me_t * share + start)
        cols = lax.broadcasted_iota(jnp.int32, (step, width), 1)
        return jnp.where((rows < dims[0, s]) & (cols < dims[1, s]), total, 0.0)

    def divided(s, start):
        return inverse_of[s, pl.ds(start, step), :]

    def part_wait(s):
        for offset in range(1, pieces):
            part_copy(s, offset).wait()

    def spread(ref, out, corr_of, meanwhile=None):
        @pl.loop(0, blocks)
        def _(s):
            for start in starts:
                value = corr_of(s, start)
                out[s, pl.ds(start, step), :] = value
                ref[blocks + s, own_rows(start), :] = value.astype(BF16)

            for offset in range(1, pieces):
                share_copy(ref, s, offset, me_t).start()
            halo_start(ref, s, 0, half)

        @pl.loop(0, blocks)
        def _(s):
            for offset in range(1, pieces):
                share_copy(ref, s, offset, term_at(pieces - offset)).wait_recv()
                halo_start(ref, s, offset, half)
            relay(ref, s, half)

        extra = meanwhile() if meanwhile is not None else None

        @pl.loop(0, blocks)
        def _(s):
            for offset in range(1, pieces):
                share_copy(ref, s, offset, me_t).wait_send()
            halo_wait(ref, s, half)
        return extra

    loads[2].wait()
    loads[3].wait()
    apply(ext1)

    def sums1(s, totals):
        part_wait(s)
        for start in starts:
            totals = sums1_rows(s, start, totals)
        return totals

    def sums1_rows(s, start, totals):
        here = pl.ds(start, step)
        sigma = masked_sum(s, start)
        sig1[s, here, :] = sigma
        inverse = divided(s, start)
        b1 = base1[s, here, :]
        r = sigma * inverse
        q = b1 * inverse
        pairs = [(b1, sigma), (b1, r), (b1, q), (r, r), (r, q), (q, q), (b1, b1)]
        return tuple(t + fold(x * y) for t, (x, y) in zip(totals, pairs))

    sum_start(1, lax.fori_loop(0, blocks, sums1, (zero,) * 7))
    got = sum_finish(1)
    theta1 = got(0)
    first_gram = got(6)
    weight = got(1) - theta1 * got(2)
    length = (
        (got(3) - 2.0 * theta1 * got(4) + theta1 * theta1 * got(5))
        - 2.0 * weight * weight
        + weight * weight * first_gram
    )
    scale1 = 1.0 / jnp.sqrt(jnp.maximum(length, 0.0) + epsilon)

    def corr1(s, start):
        here = pl.ds(start, step)
        b1 = base1[s, here, :]
        corr = (sig1[s, here, :] - theta1 * b1) * divided(s, start)
        return (corr - weight * b1) * scale1

    spread(ext2, base2, corr1)

    apply(ext2)

    def sums2(s, totals):
        part_wait(s)
        for start in starts:
            totals = sums2_rows(s, start, totals)
        return totals

    def sums2_rows(s, start, totals):
        here = pl.ds(start, step)
        sigma = masked_sum(s, start)
        sig2[s, here, :] = sigma
        inverse = divided(s, start)
        b1 = base1[s, here, :]
        b2 = base2[s, here, :]
        r = sigma * inverse
        q = b2 * inverse
        pairs = [
            (b2, sigma), (b1, r), (b2, r), (b1, q), (b2, q), (r, r), (r, q), (q, q),
            (b1, b2), (b2, b2), (b1, sigma), (b2, sig1[s, here, :]),
        ]
        return tuple(t + fold(x * y) for t, (x, y) in zip(totals, pairs))

    sum_start(2, lax.fori_loop(0, blocks, sums2, (zero,) * 12))
    more = sum_finish(2)
    theta2 = more(0)
    weight1 = more(1) - theta2 * more(3)
    weight2 = more(2) - theta2 * more(4)
    length2 = (
        (more(5) - 2.0 * theta2 * more(6) + theta2 * theta2 * more(7))
        - 2.0 * (weight1 * weight1 + weight2 * weight2)
        + weight1 * weight1 * first_gram
        + 2.0 * weight1 * weight2 * more(8)
        + weight2 * weight2 * more(9)
    )
    scale2 = 1.0 / jnp.sqrt(jnp.maximum(length2, 0.0) + epsilon)

    def corr2(s, start):
        here = pl.ds(start, step)
        b1 = base1[s, here, :]
        b2 = base2[s, here, :]
        corr = (sig2[s, here, :] - theta2 * b2) * divided(s, start)
        return (corr - weight1 * b1 - weight2 * b2) * scale2

    def cross(s, totals):
        for start in starts:
            here = pl.ds(start, step)
            b3 = last[s, here, :]
            pairs = [(b3, sig1[s, here, :]), (b3, sig2[s, here, :])]
            totals = tuple(t + fold(x * y) for t, (x, y) in zip(totals, pairs))
        return totals

    last_copy = pltpu.make_async_copy(last, last_out, load.at[0])

    def meanwhile():
        last_copy.start()
        return lax.fori_loop(0, blocks, cross, (zero,) * 2)

    crossed = spread(ext3, last, corr2, meanwhile)

    def sums3(s, totals):
        acc[s] = product(ext3, s, True)

        for start in range(0, width, step):
            here = pl.ds(start, step)
            sigma = acc[s, here, :]
            vectors = [ref[blocks + s, here, :].astype(F32) for ref in (ext1, ext2, ext3)]
            totals = tuple(t + fold(v * sigma) for t, v in zip(totals, vectors))
        return totals

    sum_start(3, list(lax.fori_loop(0, blocks, sums3, (zero,) * 3)) + list(crossed))

    def env_copy(t, s):
        return pltpu.make_async_copy(env.at[t, s], env_out.at[t, s], store.at[t, s])

    @pl.loop(0, blocks)
    def _(s):
        own = ext3[blocks + s]
        for t in range(terms):
            new = lax.dot_general(
                own, env[t, s], (((0,), (0,)), ((), ())), preferred_element_type=F32
            )
            env[t, s] = (new * width ** (-0.5)).astype(BF16)
            env_copy(t, s).start()

    end = sum_finish(3)
    cells = [
        [theta1, more(10), end(0)],
        [more(11), theta2, end(1)],
        [end(3), end(4), end(2)],
    ]
    row = lax.broadcasted_iota(jnp.int32, (8, 128), 0)
    col = lax.broadcasted_iota(jnp.int32, (8, 128), 1)
    out = zero
    for i in range(3):
        for j in range(3):
            out = jnp.where((row == i) & (col == j), cells[i][j], out)
    proj[...] = out

    @pl.loop(0, blocks)
    def _(s):
        for t in range(terms):
            env_copy(t, s).wait()

    last_copy.wait()
    for which in range(4):
        others = slots.at[which, pl.ds(0, count - 1)]
        pltpu.make_async_copy(others, others, sum_send.at[which]).wait()


def on_device(psi, left, right, connect, sector_dims, precond):
    blocks, width = psi.shape[0], psi.shape[1]
    terms = left.shape[0]
    pieces, devices = lax.axis_size("term"), lax.axis_size("sector")
    count = pieces * devices
    share = width // pieces
    entries = float(blocks * devices * width * width)
    sizes = (pieces, devices, terms, blocks, width, entries)
    others = max(pieces - 1, 1)
    dma = pltpu.SemaphoreType.DMA
    vmem = pl.BlockSpec(memory_space=pltpu.VMEM)
    smem = pl.BlockSpec(memory_space=pltpu.SMEM)
    anywhere = pl.BlockSpec(memory_space=pl.ANY)
    proj, last, env = pl.pallas_call(
        functools.partial(kernel, sizes),
        name="davidson",
        out_shape=(
            jax.ShapeDtypeStruct((8, 128), F32),
            jax.ShapeDtypeStruct((blocks, share, width), F32),
            jax.ShapeDtypeStruct((terms, blocks, width, width), BF16),
        ),
        in_specs=[smem, smem, anywhere, anywhere, anywhere, anywhere],
        out_specs=(vmem, anywhere, anywhere),
        scratch_shapes=[
            pltpu.VMEM((terms, blocks, width, width), BF16),
            pltpu.VMEM((terms, blocks, width, width), BF16),
            pltpu.VMEM((blocks, width, width), BF16),
            pltpu.VMEM((terms, blocks, width, width), BF16),
            pltpu.VMEM((blocks, width, width), BF16),
            pltpu.VMEM((blocks, share, width), F32),
            pltpu.VMEM((blocks, share, width), F32),
            pltpu.VMEM((3 * blocks, width, width), BF16),
            pltpu.VMEM((3 * blocks, width, width), BF16),
            pltpu.VMEM((3 * blocks, width, width), BF16),
            pltpu.VMEM((3 * blocks, width, width), BF16),
            pltpu.VMEM((blocks, width, width), F32),
            pltpu.VMEM((others, blocks, share, width), BF16),
            pltpu.VMEM((others, blocks, share, width), BF16),
            pltpu.VMEM((blocks, share, width), F32),
            pltpu.VMEM((blocks, share, width), F32),
            pltpu.VMEM((blocks, share, width), F32),
            pltpu.VMEM((blocks, share, width), F32),
            pltpu.VMEM((4, 1, 128), F32),
            pltpu.VMEM((4, count, 1, 128), F32),
            dma((2, pieces, blocks)),
            dma((2, pieces, blocks)),
            dma((others, blocks)),
            dma((others, blocks)),
            dma((others, blocks)),
            dma((others, blocks)),
            dma((others, blocks)),
            dma((4,)),
            dma((4,)),
            dma((4,)),
            dma((terms, blocks)),
        ],
        compiler_params=pltpu.CompilerParams(
            collective_id=0, has_side_effects=True, vmem_limit_bytes=60 * 1024 * 1024
        ),
    )(sector_dims, connect, psi, left, right, precond)
    return proj[:3, :3], last, env


def solution(mesh):
    placed = (
        P("sector", None, None),
        P("term", "sector", None, None),
        P("term", "sector", None, None),
        P("term", "sector"),
        P(None, "sector"),
        P("sector", None, None),
    )
    return jax.shard_map(
        on_device,
        mesh=mesh,
        in_specs=placed,
        out_specs=(P(), P("sector", "term", None), P("term", "sector", None, None)),
        check_vma=False,
    )
```

profile of v0, /device:TPU:0, one launch (start us, length us, event | category | flops | bytes accessed | tf_op | source)
XLA Modules:
  0.0 113.9 jit_solution(13971526279526680476)
XLA Ops:
  0.6 105.9 %davidson.1 = (f32[8,128]{1,0:T(8,128)}, f32[8,128,256]{2,1,0:T(8,128)}, bf16[3,8,256,256]{3,2,1,0:T(8,128)(2,1)}) custom-call(s32[2,8]{1,0:T(2,128)} %dims.1, s32[3,8]{1,0:T(4,128)} %conn.1, bf16[8,256,256]{2,1,0:T(8,128)(2,1)} %psi_in.1, bf16[3,8,256,256]{3,2,1,0:T(8,128)(2,1)} %left_in.1, bf16[3,8,256,256]{3,2,1,0:T(8,128)(2,1)} %right_in.1, ...), custom_call_target="tpu_custom_call" | custom-call | tf_op jit(solution)/shard_map/davidson/pallas_call | solution.py:499
  106.5 1.3 %slice.3 = f32[3,3]{1,0:T(4,128)} slice(f32[8,128]{1,0:T(8,128)} %get-tuple-element.6), slice={[0:3], [0:3]} | slice | bytes 72 | tf_op jit(solution)/shard_map/slice | solution.py:546
  107.8 2.3 %copy.11 = f32[8,128,256]{2,1,0:T(8,128)} copy(f32[8,128,256]{2,1,0:T(8,128)} %get-tuple-element.13) | data formatting | bytes 2097152
  110.0 3.9 %copy.12 = bf16[3,8,256,256]{3,2,1,0:T(8,128)(2,1)} copy(bf16[3,8,256,256]{3,2,1,0:T(8,128)(2,1)} %get-tuple-element.14) | data formatting | bytes 6291456
where the time goes:
time: 114 us
  Pallas kernels  106 us (93%)
  local copies, waits for them, and re-layouts  7.38 us (6%)
    pallas_call x1, Pallas kernels, on_device(): pl.pallas_call(functools.partial(kernel, sizes), name='davidson', out_sha...  106 us
    unnamed x2, local copies, waits for them, and re-layouts  6.12 us

commit v1 on v0

v1 whole, which is shorter than its diff:
```python
import functools
import jax
import jax.numpy as jnp
from jax import lax
from jax.experimental import pallas as pl
from jax.experimental.pallas import tpu as pltpu
from jax.sharding import PartitionSpec as P

epsilon = 1e-06
MESH = pl.DeviceIdType.MESH
F32 = jnp.float32
BF16 = jnp.bfloat16


def fold(values):
    rows, width = values.shape
    total = values.reshape(rows // 8, 8, width).sum(axis=0)
    out = total[:, :128]
    for start in range(128, width, 128):
        out = out + total[:, start : start + 128]
    return out


def rounds_of(devices):
    out, stride = [], 1
    while stride < devices:
        radix = 4 if devices // stride % 4 == 0 else 2
        out.append((stride, radix))
        stride *= radix
    return out


def kernel(
    sizes, relays,
    dims, conn, psi_in, left_in, right_in, pre_in,
    proj, last, env,
    left, right, pre, psi, inverse_of, raw, far1, far2, far3, ext1, ext2, ext3, acc, stage, came, sig1, sig2, base1, base2,
    tile, slots, norm_tile, norm_slots,
    on_send, on_recv, off_send, off_recv, relay_send, share_send, share_recv, part_send, part_recv,
    sum_send, sum_recv, norm_send, norm_recv, load,
):
    pieces, devices, terms, blocks, width, entries = sizes
    share = width // pieces
    count = pieces * devices
    step = min(32, share)
    steps = share // step
    me_t = lax.axis_index("term")
    me_s = lax.axis_index("sector")
    me = me_t * devices + me_s
    first = me_s * blocks - blocks
    odd = lax.rem(me_s, 2)
    on_s = me_s + 1 - 2 * odd
    off_s = me_s - 1 + 2 * odd
    has_off = (off_s >= 0) & (off_s < devices)
    zero = jnp.zeros((8, 128), F32)
    rounds = rounds_of(devices)

    def order(k):
        return k + odd * (blocks - 1 - 2 * k)

    def turn(k):
        return blocks - 1 - k + odd * (2 * k - blocks + 1)

    def device_at(offset):
        other = lax.rem(me + offset, count)
        return (other // devices, lax.rem(other, devices))

    def term_at(offset):
        return lax.rem(me_t + offset, pieces)

    def rows_of(piece):
        return pl.ds(pl.multiple_of(piece * share, share), share)

    def part_rows(j):
        return rows_of(term_at(pieces - j))

    everything = pl.ds(0, width)

    def arrived(view, sem):
        pltpu.make_async_copy(view, view, sem).wait()

    loads = [
        pltpu.make_async_copy(source, target, load.at[i])
        for i, (source, target) in enumerate(
            ((psi_in, psi), (pre_in, pre), (left_in, left), (right_in, right))
        )
    ]
    loads[0].start()

    barrier = pltpu.get_barrier_semaphore()

    def greet(t, s):
        pl.semaphore_signal(barrier, inc=1, device_id=(t, s), device_id_type=MESH)

    def peers(stride, radix):
        digit = lax.rem(me_s // stride, radix)
        return digit, [
            me_s + (lax.rem(digit + d, radix) - digit) * stride for d in range(1, radix)
        ]

    greeted = pieces - 1
    for stride, radix in rounds:
        for other in peers(stride, radix)[1]:
            greet(me_t, other)
        greeted += radix - 1
    for j in range(1, pieces):
        greet(term_at(j), me_s)
    apart = has_off & (off_s // rounds[0][1] != me_s // rounds[0][1])

    @pl.when(apart)
    def _():
        greet(me_t, off_s)

    loads[0].wait()
    for one in loads[1:]:
        one.start()

    pl.semaphore_wait(barrier, greeted + apart.astype(jnp.int32))

    def on_copy(ref, s, j, rows):
        return pltpu.make_async_remote_copy(
            src_ref=ref.at[blocks + s, rows],
            dst_ref=ref.at[s + odd * 2 * blocks, rows],
            send_sem=on_send.at[j, s],
            recv_sem=on_recv.at[j, s],
            device_id=(me_t, on_s),
            device_id_type=MESH,
        )

    def on_arrived(ref, s, j, rows):
        arrived(ref.at[s + (1 - odd) * 2 * blocks, rows], on_recv.at[j, s])

    def off_copy(ref, far, s, j):
        return pltpu.make_async_remote_copy(
            src_ref=ref.at[blocks + s, part_rows(j)],
            dst_ref=far.at[s, part_rows(j)],
            send_sem=off_send.at[j, s],
            recv_sem=off_recv.at[j, s],
            device_id=(me_t, off_s),
            device_id_type=MESH,
        )

    def off_slot(s):
        return s + odd * 2 * blocks

    def off_arrived(far, s, j):
        arrived(far.at[s, part_rows(j)], off_recv.at[j, s])

    def relay_copy(far, s, j):
        return pltpu.make_async_remote_copy(
            src_ref=far.at[s, rows_of(me_t)],
            dst_ref=far.at[s, rows_of(me_t)],
            send_sem=relay_send.at[j - 1, s],
            recv_sem=off_recv.at[j, s],
            device_id=(term_at(j), me_s),
            device_id_type=MESH,
        )

    def relayed(k, span):
        return (k >= span[0]) & (k < span[1])

    def relay(far, k, span):
        @pl.when(has_off & relayed(k, span))
        def _():
            s = turn(k)
            off_arrived(far, s, 0)
            for j in range(1, pieces):
                relay_copy(far, s, j).start()

    def receive(far, k, span):
        s = turn(k)

        @pl.when(has_off & jnp.logical_not(relayed(k, span)))
        def _():
            off_arrived(far, s, 0)

        @pl.when(has_off)
        def _():
            for j in range(1, pieces):
                off_arrived(far, s, j)

    def sent(ref, far, span, whole):
        @pl.loop(0, blocks)
        def _(k):
            s = order(k)
            if whole:
                on_copy(ref, s, 0, everything).wait_send()
            else:
                for j in range(pieces):
                    on_copy(ref, s, j, part_rows(j)).wait_send()
                for offset in range(1, pieces):
                    share_copy(ref, s, offset, me_t).wait_send()

            @pl.when(has_off)
            def _():
                off_copy(ref, far, s, 0).wait_send()

            @pl.when(has_off & jnp.logical_not(relayed(k, span)))
            def _():
                for j in range(1, pieces):
                    off_copy(ref, far, s, j).wait_send()

            @pl.when(has_off & relayed(k, span))
            def _():
                for j in range(1, pieces):
                    relay_copy(far, turn(k), j).wait_send()

    def share_copy(ref, s, offset, piece):
        return pltpu.make_async_remote_copy(
            src_ref=ref.at[blocks + s, rows_of(piece)],
            dst_ref=ref.at[blocks + s, rows_of(piece)],
            send_sem=share_send.at[offset - 1, s],
            recv_sem=share_recv.at[offset - 1, s],
            device_id=(term_at(offset), me_s),
            device_id_type=MESH,
        )

    def part_copy(s, offset):
        return pltpu.make_async_remote_copy(
            src_ref=stage.at[offset - 1, s],
            dst_ref=came.at[offset - 1, s],
            send_sem=part_send.at[offset - 1, s],
            recv_sem=part_recv.at[offset - 1, s],
            device_id=(term_at(offset), me_s),
            device_id_type=MESH,
        )

    lane = lax.broadcasted_iota(jnp.int32, (1, 128), 1)

    def pack(tiles):
        packed = jnp.zeros((1, 128), F32)
        for i, one in enumerate(tiles):
            row = jnp.sum(one, axis=0, keepdims=True)
            packed = jnp.where(lane == i, jnp.sum(row, axis=1, keepdims=True), packed)
        return packed

    def sum_start(which, tiles):
        packed = pack(tiles)
        tile[which] = packed
        slots[which, me] = packed

        @pl.loop(1, count)
        def _(offset):
            pltpu.make_async_remote_copy(
                src_ref=tile.at[which],
                dst_ref=slots.at[which, me],
                send_sem=sum_send.at[which],
                recv_sem=sum_recv.at[which],
                device_id=device_at(offset),
                device_id_type=MESH,
            ).start()

    def sum_finish(which):
        others = slots.at[which, pl.ds(0, count - 1)]
        arrived(others, sum_recv.at[which])
        full = jnp.sum(slots[which], axis=0) / entries
        return lambda i: full[:, i : i + 1]

    def norm_start(i, packed):
        digit, others = peers(*rounds[i])
        norm_tile[i] = packed
        norm_slots[i, digit] = packed
        for other in others:
            pltpu.make_async_remote_copy(
                src_ref=norm_tile.at[i],
                dst_ref=norm_slots.at[i, digit],
                send_sem=norm_send.at[i],
                recv_sem=norm_recv.at[i],
                device_id=(me_t, other),
                device_id_type=MESH,
            ).start()

    def norm_finish(i):
        radix = rounds[i][1]
        arrived(norm_slots.at[i, pl.ds(0, radix - 1)], norm_recv.at[i])
        return jnp.sum(norm_slots[i, pl.ds(0, radix)], axis=0)

    starts = [k * step for k in range(steps)]
    strips = list(range(0, width, step))

    def own_rows(start):
        return pl.ds(pl.multiple_of(me_t * share + start, step), step)

    span0 = relays[0]

    def first_step(k, total):
        s = order(k)
        for start in strips:
            here = pl.ds(start, step)
            rows = lax.broadcasted_iota(jnp.int32, (step, width), 0) + start
            cols = lax.broadcasted_iota(jnp.int32, (step, width), 1)
            keep = (rows < dims[0, s]) & (cols < dims[1, s])
            v = jnp.where(keep, psi[s, here, :].astype(F32), 0.0)
            raw[blocks + s, here, :] = v.astype(BF16)
            total = total + fold(v * v)
        return total

    norm_start(0, pack([lax.fori_loop(0, blocks, first_step, zero)]))

    @pl.loop(0, blocks)
    def _(k):
        s = order(k)
        on_copy(raw, s, 0, everything).start()

        @pl.when(has_off)
        def _():
            off_copy(raw, far1, s, 0).start()

        @pl.when(has_off & jnp.logical_not(relayed(k, span0)))
        def _():
            for j in range(1, pieces):
                off_copy(raw, far1, s, j).start()

    loads[1].wait()

    @pl.loop(0, blocks)
    def _(s):
        for start in starts:
            inverse_of[s, pl.ds(start, step), :] = 1.0 / pre[s, own_rows(start), :].astype(F32)

    total = None
    for i in range(len(rounds)):
        total = norm_finish(i)
        if i + 1 < len(rounds):
            norm_start(i + 1, total)
        if i == 0:
            for k in range(relays[0][2]):
                relay(far1, k, span0)
    norm = total[:, 0:1] / entries
    scale = 1.0 / jnp.sqrt(norm + epsilon)

    def scaled(source, place, slot):
        for start in strips:
            here = pl.ds(start, step)
            ext1[slot, here, :] = (source[place, here, :].astype(F32) * scale).astype(BF16)

    @pl.loop(0, blocks)
    def _(s):
        scaled(raw, blocks + s, blocks + s)
        for start in starts:
            base1[s, pl.ds(start, step), :] = raw[blocks + s, own_rows(start), :].astype(F32) * scale

    @pl.loop(0, blocks)
    def _(k):
        s = turn(k)
        on_arrived(raw, s, 0, everything)
        slot = s + (1 - odd) * 2 * blocks
        scaled(raw, slot, slot)

    def product(ref, s, keep):
        halves = []
        for t in range(terms):
            source = ref[jnp.clip(conn[t, s] - first, 0, 3 * blocks - 1)]
            one = jnp.dot(left[t, s], source, preferred_element_type=F32).astype(BF16)
            halves.append(one)
            if keep:
                env[t, s] = one
        total = None
        for t in range(terms):
            one = lax.dot_general(
                halves[t], right[t, s], (((1,), (1,)), ((), ())), preferred_element_type=F32
            )
            total = one if total is None else total + one
        return total

    def take(ref, far, k, span, scaling):
        s = turn(k)
        relay(far, k + span[2], span)
        receive(far, k, span)

        @pl.when(has_off)
        def _():
            if scaling:
                scaled(far, s, off_slot(s))
            else:
                ref[off_slot(s)] = far[s]

    def apply(ref, far, span, scaling):
        @pl.loop(0, blocks)
        def _(k):
            take(ref, far, k, span, scaling)
            s = turn(k)
            acc[s] = product(ref, s, False)
            for offset in range(1, pieces):
                stage[offset - 1, s] = acc[s, rows_of(term_at(offset)), :].astype(BF16)
                part_copy(s, offset).start()

    def masked_sum(s, start):
        total = acc[s, own_rows(start), :]
        for offset in range(1, pieces):
            total = total + came[offset - 1, s, pl.ds(start, step), :].astype(F32)
        rows = lax.broadcasted_iota(jnp.int32, (step, width), 0) + (me_t * share + start)
        cols = lax.broadcasted_iota(jnp.int32, (step, width), 1)
        return jnp.where((rows < dims[0, s]) & (cols < dims[1, s]), total, 0.0)

    def divided(s, start):
        return inverse_of[s, pl.ds(start, step), :]

    def part_wait(s):
        for offset in range(1, pieces):
            part_copy(s, offset).wait()

    def spread(ref, far, out, corr_of, span):
        @pl.loop(0, blocks)
        def _(k):
            s = order(k)
            for start in starts:
                value = corr_of(s, start)
                out[s, pl.ds(start, step), :] = value
                ref[blocks + s, own_rows(start), :] = value.astype(BF16)

            for offset in range(1, pieces):
                share_copy(ref, s, offset, me_t).start()
            on_copy(ref, s, 0, part_rows(0)).start()

            @pl.when(has_off)
            def _():
                off_copy(ref, far, s, 0).start()

        @pl.loop(0, blocks)
        def _(k):
            s = order(k)
            for offset in range(1, pieces):
                arrived(ref.at[blocks + s, part_rows(offset)], share_recv.at[offset - 1, s])
                on_copy(ref, s, offset, part_rows(offset)).start()

                @pl.when(has_off & jnp.logical_not(relayed(k, span)))
                def _():
                    off_copy(ref, far, s, offset).start()

        for k in range(span[2]):
            relay(far, k, span)

    def settle(ref):
        @pl.loop(0, blocks)
        def _(k):
            s = turn(k)
            for j in range(pieces):
                on_arrived(ref, s, j, part_rows(j))

    loads[2].wait()
    loads[3].wait()
    apply(ext1, far1, span0, True)

    def sums1(k, totals):
        s = turn(k)
        part_wait(s)
        for start in starts:
            totals = sums1_rows(s, start, totals)
        return totals

    def sums1_rows(s, start, totals):
        here = pl.ds(start, step)
        sigma = masked_sum(s, start)
        sig1[s, here, :] = sigma
        inverse = divided(s, start)
        b1 = base1[s, here, :]
        r = sigma * inverse
        q = b1 * inverse
        pairs = [(b1, sigma), (b1, r), (b1, q), (r, r), (r, q), (q, q), (b1, b1)]
        return tuple(t + fold(x * y) for t, (x, y) in zip(totals, pairs))

    sum_start(0, lax.fori_loop(0, blocks, sums1, (zero,) * 7))
    sent(raw, far1, span0, True)
    got = sum_finish(0)
    theta1 = got(0)
    first_gram = got(6)
    weight = got(1) - theta1 * got(2)
    length = (
        (got(3) - 2.0 * theta1 * got(4) + theta1 * theta1 * got(5))
        - 2.0 * weight * weight
        + weight * weight * first_gram
    )
    scale1 = 1.0 / jnp.sqrt(jnp.maximum(length, 0.0) + epsilon)

    def corr1(s, start):
        here = pl.ds(start, step)
        b1 = base1[s, here, :]
        corr = (sig1[s, here, :] - theta1 * b1) * divided(s, start)
        return (corr - weight * b1) * scale1

    spread(ext2, far2, base2, corr1, relays[1])
    settle(ext2)
    apply(ext2, far2, relays[1], False)

    def sums2(k, totals):
        s = turn(k)
        part_wait(s)
        for start in starts:
            totals = sums2_rows(s, start, totals)
        return totals

    def sums2_rows(s, start, totals):
        here = pl.ds(start, step)
        sigma = masked_sum(s, start)
        sig2[s, here, :] = sigma
        inverse = divided(s, start)
        b1 = base1[s, here, :]
        b2 = base2[s, here, :]
        r = sigma * inverse
        q = b2 * inverse
        pairs = [
            (b2, sigma), (b1, r), (b2, r), (b1, q), (b2, q), (r, r), (r, q), (q, q),
            (b1, b2), (b2, b2), (b1, sigma), (b2, sig1[s, here, :]),
        ]
        return tuple(t + fold(x * y) for t, (x, y) in zip(totals, pairs))

    sum_start(1, lax.fori_loop(0, blocks, sums2, (zero,) * 12))
    sent(ext2, far2, relays[1], False)
    more = sum_finish(1)
    theta2 = more(0)
    weight1 = more(1) - theta2 * more(3)
    weight2 = more(2) - theta2 * more(4)
    length2 = (
        (more(5) - 2.0 * theta2 * more(6) + theta2 * theta2 * more(7))
        - 2.0 * (weight1 * weight1 + weight2 * weight2)
        + weight1 * weight1 * first_gram
        + 2.0 * weight1 * weight2 * more(8)
        + weight2 * weight2 * more(9)
    )
    scale2 = 1.0 / jnp.sqrt(jnp.maximum(length2, 0.0) + epsilon)

    def corr2(s, start):
        here = pl.ds(start, step)
        b1 = base1[s, here, :]
        b2 = base2[s, here, :]
        corr = (sig2[s, here, :] - theta2 * b2) * divided(s, start)
        return (corr - weight1 * b1 - weight2 * b2) * scale2

    def cross(s, totals):
        for start in starts:
            here = pl.ds(start, step)
            b3 = last[s, here, :]
            pairs = [(b3, sig1[s, here, :]), (b3, sig2[s, here, :])]
            totals = tuple(t + fold(x * y) for t, (x, y) in zip(totals, pairs))
        return totals

    spread(ext3, far3, last, corr2, relays[2])
    crossed = lax.fori_loop(0, blocks, cross, (zero,) * 2)
    settle(ext3)

    def sums3(k, totals):
        take(ext3, far3, k, relays[2], False)
        s = turn(k)
        acc[s] = product(ext3, s, True)

        for start in strips:
            here = pl.ds(start, step)
            sigma = acc[s, here, :]
            vectors = [ref[blocks + s, here, :].astype(F32) for ref in (ext1, ext2, ext3)]
            totals = tuple(t + fold(v * sigma) for t, v in zip(totals, vectors))
        return totals

    sum_start(2, list(lax.fori_loop(0, blocks, sums3, (zero,) * 3)) + list(crossed))

    @pl.loop(0, blocks)
    def _(s):
        own = ext3[blocks + s]
        for t in range(terms):
            new = lax.dot_general(
                own, env[t, s], (((0,), (0,)), ((), ())), preferred_element_type=F32
            )
            env[t, s] = (new * width ** (-0.5)).astype(BF16)

    sent(ext3, far3, relays[2], False)
    end = sum_finish(2)
    cells = [
        [theta1, more(10), end(0)],
        [more(11), theta2, end(1)],
        [end(3), end(4), end(2)],
    ]
    row = lax.broadcasted_iota(jnp.int32, (8, 128), 0)
    col = lax.broadcasted_iota(jnp.int32, (8, 128), 1)
    out = zero
    for i in range(3):
        for j in range(3):
            out = jnp.where((row == i) & (col == j), cells[i][j], out)
    proj[...] = out

    for which in range(3):
        arrived(slots.at[which, pl.ds(0, count - 1)], sum_send.at[which])
    for i, (stride, radix) in enumerate(rounds):
        arrived(norm_slots.at[i, pl.ds(0, radix - 1)], norm_send.at[i])


def write_kernel(proj, last, env, proj_out, last_out, env_out, sem):
    copies = [
        pltpu.make_async_copy(last, last_out, sem.at[0]),
        pltpu.make_async_copy(env, env_out, sem.at[1]),
    ]
    for one in copies:
        one.start()
    proj_out[...] = proj[:3, :3]
    for one in copies:
        one.wait()


def write(proj, last, env):
    vmem = pl.BlockSpec(memory_space=pltpu.VMEM)
    anywhere = pl.BlockSpec(memory_space=pl.ANY)
    hbm = pl.BlockSpec(memory_space=pltpu.HBM)
    return pl.pallas_call(
        write_kernel,
        name="write",
        out_shape=(
            jax.ShapeDtypeStruct((3, 3), F32),
            jax.ShapeDtypeStruct(last.shape, F32),
            jax.ShapeDtypeStruct(env.shape, BF16),
        ),
        in_specs=[vmem, anywhere, anywhere],
        out_specs=(vmem, hbm, hbm),
        scratch_shapes=[pltpu.SemaphoreType.DMA((2,))],
        compiler_params=pltpu.CompilerParams(vmem_limit_bytes=12 * 1024 * 1024),
    )(proj, last, env)


RELAYS = ((0, 4, 2), (7, 8, 4), (4, 8, 4))


def on_device(psi, left, right, connect, sector_dims, precond):
    blocks, width = psi.shape[0], psi.shape[1]
    terms = left.shape[0]
    pieces, devices = lax.axis_size("term"), lax.axis_size("sector")
    count = pieces * devices
    share = width // pieces
    entries = float(blocks * devices * width * width)
    sizes = (pieces, devices, terms, blocks, width, entries)
    others = max(pieces - 1, 1)
    rounds = len(rounds_of(devices))
    dma = pltpu.SemaphoreType.DMA
    vmem = pl.BlockSpec(memory_space=pltpu.VMEM)
    smem = pl.BlockSpec(memory_space=pltpu.SMEM)
    hbm = pl.BlockSpec(memory_space=pltpu.HBM)
    operands = [
        pltpu.with_memory_space_constraint(one, pltpu.HBM)
        for one in (sector_dims, connect, psi, left, right, precond)
    ]
    proj, last, env = pl.pallas_call(
        functools.partial(kernel, sizes, RELAYS),
        name="davidson",
        out_shape=(
            jax.ShapeDtypeStruct((8, 128), F32),
            pltpu.VMEM((blocks, share, width), F32),
            pltpu.VMEM((terms, blocks, width, width), BF16),
        ),
        in_specs=[smem, smem, hbm, hbm, hbm, hbm],
        out_specs=(vmem, vmem, vmem),
        scratch_shapes=[
            pltpu.VMEM((terms, blocks, width, width), BF16),
            pltpu.VMEM((terms, blocks, width, width), BF16),
            pltpu.VMEM((blocks, width, width), BF16),
            pltpu.VMEM((blocks, width, width), BF16),
            pltpu.VMEM((blocks, share, width), F32),
            pltpu.VMEM((3 * blocks, width, width), BF16),
            pltpu.VMEM((blocks, width, width), BF16),
            pltpu.VMEM((blocks, width, width), BF16),
            pltpu.VMEM((blocks, width, width), BF16),
            pltpu.VMEM((3 * blocks, width, width), BF16),
            pltpu.VMEM((3 * blocks, width, width), BF16),
            pltpu.VMEM((3 * blocks, width, width), BF16),
            pltpu.VMEM((blocks, width, width), F32),
            pltpu.VMEM((others, blocks, share, width), BF16),
            pltpu.VMEM((others, blocks, share, width), BF16),
            pltpu.VMEM((blocks, share, width), F32),
            pltpu.VMEM((blocks, share, width), F32),
            pltpu.VMEM((blocks, share, width), F32),
            pltpu.VMEM((blocks, share, width), F32),
            pltpu.VMEM((3, 1, 128), F32),
            pltpu.VMEM((3, count, 1, 128), F32),
            pltpu.VMEM((rounds, 1, 128), F32),
            pltpu.VMEM((rounds, 4, 1, 128), F32),
            dma((pieces, blocks)),
            dma((pieces, blocks)),
            dma((pieces, blocks)),
            dma((pieces, blocks)),
            dma((others, blocks)),
            dma((others, blocks)),
            dma((others, blocks)),
            dma((others, blocks)),
            dma((others, blocks)),
            dma((3,)),
            dma((3,)),
            dma((rounds,)),
            dma((rounds,)),
            dma((4,)),
        ],
        compiler_params=pltpu.CompilerParams(
            collective_id=0, has_side_effects=True, vmem_limit_bytes=48 * 1024 * 1024
        ),
    )(*operands)
    return write(proj, last, env)


def solution(mesh):
    placed = (
        P("sector", None, None),
        P("term", "sector", None, None),
        P("term", "sector", None, None),
        P("term", "sector"),
        P(None, "sector"),
        P("sector", None, None),
    )
    return jax.shard_map(
        on_device,
        mesh=mesh,
        in_specs=placed,
        out_specs=(P(), P("sector", "term", None), P("term", "sector", None, None)),
        check_vma=False,
    )
```

time: 114 us -> 105 us (0.921)
  local copies, waits for them, and re-layouts: 7.38 us -> 0 us
  Pallas kernels: 106 us -> 104 us
    unnamed x2 -> x0, local copies, waits for them, and re-layouts: 6.12 us -> none
    pallas_call x1 -> x2, Pallas kernels: 106 us -> 104 us  [the longest x1 101 us: on_device(): pl.pallas_call(functools.partial(kernel, sizes, RELAYS), name='davidson',...]
    slice x1 -> x0, local copies, waits for them, and re-layouts: 1.25 us -> none  [on_device(): return (proj[:3, :3], last, env)]
where the time goes in v1:
time: 105 us
  Pallas kernels  104 us (99%)
    pallas_call x1, Pallas kernels, on_device(): pl.pallas_call(functools.partial(kernel, sizes, RELAYS), name='davidson',...  101 us
    pallas_call x1, Pallas kernels, write(): pl.pallas_call(write_kernel, name='write', out_shape=(jax.ShapeDtypeStruc...  2.61 us

profile of v1, /device:TPU:0, one launch (start us, length us, event | category | flops | bytes accessed | tf_op | source)
XLA Modules:
  0.0 104.6 jit_solution(16776138917247090245)
XLA Ops:
  0.6 101.4 %davidson.1 = (f32[8,128]{1,0:T(8,128)S(1)}, f32[8,128,256]{2,1,0:T(8,128)S(1)}, bf16[3,8,256,256]{3,2,1,0:T(8,128)(2,1)S(1)}) custom-call(s32[2,8]{1,0:T(2,128)} %dims.1, s32[3,8]{1,0:T(4,128)} %conn.1, bf16[8,256,256]{2,1,0:T(8,128)(2,1)} %psi_in.1, bf16[3,8,256,256]{3,2,1,0:T(8,128)(2,1)} %left_in.1, bf16[3,8,256,256]{3,2,1,0:T(8,128)(2,1)} %right_in.1, ...), custom_call_target="tpu_custom_call" | custom-call | tf_op jit(solution)/shard_map/davidson/pallas_call | solution.py:638
  102.0 2.6 %write.1 = (f32[3,3]{1,0:T(4,128)}, f32[8,128,256]{2,1,0:T(8,128)}, bf16[3,8,256,256]{3,2,1,0:T(8,128)(2,1)}) custom-call(f32[8,128]{1,0:T(8,128)S(1)} %get-tuple-element.6.proj, f32[8,128,256]{2,1,0:T(8,128)S(1)} %get-tuple-element.7.last, bf16[3,8,256,256]{3,2,1,0:T(8,128)(2,1)S(1)} %get-tuple-element.8.env), custom_call_target="tpu_custom_call" | custom-call | tf_op jit(solution)/shard_map/write/pallas_call | solution.py:602

commit v2 on v1

--- a/solution.py
+++ b/solution.py
@@ -34,10 +34,10 @@
     sizes, relays,
     dims, conn, psi_in, left_in, right_in, pre_in,
     proj, last, env,
-    left, right, pre, psi, inverse_of, raw, far1, far2, far3, ext1, ext2, ext3, acc, stage, came, sig1, sig2, base1, base2,
-    tile, slots, norm_tile, norm_slots,
-    on_send, on_recv, off_send, off_recv, relay_send, share_send, share_recv, part_send, part_recv,
-    sum_send, sum_recv, norm_send, norm_recv, load,
+    left, right, pre, psi, inverse_of, raw, far1, far2, far3, ext1, ext2, ext3, acc, stage, came, mine, given, other2, sig1, sig2, base1, base2,
+    tile, slots, term_tile, term_slots, norm_tile, norm_slots,
+    on_send, on_recv, off_send, off_recv, relay_send, share_send, share_recv, mine_send, mine_recv, part_send, part_recv,
+    sum_send, sum_recv, term_send, term_recv, norm_send, norm_recv, load,
 ):
     pieces, devices, terms, blocks, width, entries = sizes
     share = width // pieces
@@ -48,6 +48,7 @@
     me_s = lax.axis_index("sector")
     me = me_t * devices + me_s
     first = me_s * blocks - blocks
+    paired = pieces == 2
     odd = lax.rem(me_s, 2)
     on_s = me_s + 1 - 2 * odd
     off_s = me_s - 1 + 2 * odd
@@ -115,7 +116,6 @@
     for one in loads[1:]:
         one.start()
 
-    pl.semaphore_wait(barrier, greeted + apart.astype(jnp.int32))
 
     def on_copy(ref, s, j, rows):
         return pltpu.make_async_remote_copy(
@@ -188,8 +188,9 @@
             else:
                 for j in range(pieces):
                     on_copy(ref, s, j, part_rows(j)).wait_send()
-                for offset in range(1, pieces):
-                    share_copy(ref, s, offset, me_t).wait_send()
+                if not paired:
+                    for offset in range(1, pieces):
+                        share_copy(ref, s, offset, me_t).wait_send()
 
             @pl.when(has_off)
             def _():
@@ -215,6 +216,16 @@
             device_id_type=MESH,
         )
 
+    def mine_copy(which, s):
+        return pltpu.make_async_remote_copy(
+            src_ref=mine.at[s],
+            dst_ref=given.at[which, s],
+            send_sem=mine_send.at[which, s],
+            recv_sem=mine_recv.at[which, s],
+            device_id=(term_at(1), me_s),
+            device_id_type=MESH,
+        )
+
     def part_copy(s, offset):
         return pltpu.make_async_remote_copy(
             src_ref=stage.at[offset - 1, s],
@@ -233,6 +244,37 @@
             row = jnp.sum(one, axis=0, keepdims=True)
             packed = jnp.where(lane == i, jnp.sum(row, axis=1, keepdims=True), packed)
         return packed
+
+    def term_start(which, tiles):
+        packed = pack(tiles)
+        term_tile[which] = packed
+        term_slots[which, me_t] = packed
+        for offset in range(1, pieces):
+            pltpu.make_async_remote_copy(
+                src_ref=term_tile.at[which],
+                dst_ref=term_slots.at[which, me_t],
+                send_sem=term_send.at[which],
+                recv_sem=term_recv.at[which],
+                device_id=(term_at(offset), me_s),
+                device_id_type=MESH,
+            ).start()
+
+    def sector_start(which):
+        arrived(term_slots.at[which, pl.ds(0, pieces - 1)], term_recv.at[which])
+        packed = jnp.sum(term_slots[which], axis=0)
+        tile[which] = packed
+        slots[which, me_s] = packed
+
+        @pl.loop(1, devices)
+        def _(offset):
+            pltpu.make_async_remote_copy(
+                src_ref=tile.at[which],
+                dst_ref=slots.at[which, me_s],
+                send_sem=sum_send.at[which],
+                recv_sem=sum_recv.at[which],
+                device_id=(me_t, lax.rem(me_s + offset, devices)),
+                device_id_type=MESH,
+            ).start()
 
     def sum_start(which, tiles):
         packed = pack(tiles)
@@ -250,10 +292,10 @@
                 device_id_type=MESH,
             ).start()
 
-    def sum_finish(which):
-        others = slots.at[which, pl.ds(0, count - 1)]
+    def sum_finish(which, members):
+        others = slots.at[which, pl.ds(0, members - 1)]
         arrived(others, sum_recv.at[which])
-        full = jnp.sum(slots[which], axis=0) / entries
+        full = jnp.sum(slots[which, pl.ds(0, members)], axis=0) / entries
         return lambda i: full[:, i : i + 1]
 
     def norm_start(i, packed):
@@ -295,7 +337,9 @@
             total = total + fold(v * v)
         return total
 
-    norm_start(0, pack([lax.fori_loop(0, blocks, first_step, zero)]))
+    own_norm = pack([lax.fori_loop(0, blocks, first_step, zero)])
+    pl.semaphore_wait(barrier, greeted + apart.astype(jnp.int32))
+    norm_start(0, own_norm)
 
     @pl.loop(0, blocks)
     def _(k):
@@ -315,8 +359,9 @@
 
     @pl.loop(0, blocks)
     def _(s):
-        for start in starts:
-            inverse_of[s, pl.ds(start, step), :] = 1.0 / pre[s, own_rows(start), :].astype(F32)
+        for start in strips:
+            here = pl.ds(start, step)
+            inverse_of[s, here, :] = 1.0 / pre[s, here, :].astype(F32)
 
     total = None
     for i in range(len(rounds)):
@@ -385,22 +430,42 @@
                 stage[offset - 1, s] = acc[s, rows_of(term_at(offset)), :].astype(BF16)
                 part_copy(s, offset).start()
 
+    def masked(s, base, total):
+        rows = lax.broadcasted_iota(jnp.int32, (step, width), 0) + base
+        cols = lax.broadcasted_iota(jnp.int32, (step, width), 1)
+        return jnp.where((rows < dims[0, s]) & (cols < dims[1, s]), total, 0.0)
+
     def masked_sum(s, start):
         total = acc[s, own_rows(start), :]
         for offset in range(1, pieces):
             total = total + came[offset - 1, s, pl.ds(start, step), :].astype(F32)
-        rows = lax.broadcasted_iota(jnp.int32, (step, width), 0) + (me_t * share + start)
-        cols = lax.broadcasted_iota(jnp.int32, (step, width), 1)
-        return jnp.where((rows < dims[0, s]) & (cols < dims[1, s]), total, 0.0)
+        return masked(s, me_t * share + start, total)
+
+    def other_rows(start):
+        return pl.ds(pl.multiple_of(term_at(1) * share + start, step), step)
+
+    def other_sum(which, s, start):
+        total = acc[s, other_rows(start), :] + given[which, s, pl.ds(start, step), :].astype(F32)
+        return masked(s, term_at(1) * share + start, total)
+
+    def give(which):
+        if not paired:
+            return
+
+        @pl.loop(0, blocks)
+        def _(k):
+            s = order(k)
+            mine[s] = acc[s, rows_of(me_t), :].astype(BF16)
+            mine_copy(which, s).start()
 
     def divided(s, start):
-        return inverse_of[s, pl.ds(start, step), :]
+        return inverse_of[s, own_rows(start), :]
 
     def part_wait(s):
         for offset in range(1, pieces):
             part_copy(s, offset).wait()
 
-    def spread(ref, far, out, corr_of, span):
+    def spread(which, ref, far, out, corr_of, other_of, span):
         @pl.loop(0, blocks)
         def _(k):
             s = order(k)
@@ -409,27 +474,42 @@
                 out[s, pl.ds(start, step), :] = value
                 ref[blocks + s, own_rows(start), :] = value.astype(BF16)
 
-            for offset in range(1, pieces):
-                share_copy(ref, s, offset, me_t).start()
+            if not paired:
+                for offset in range(1, pieces):
+                    share_copy(ref, s, offset, me_t).start()
             on_copy(ref, s, 0, part_rows(0)).start()
 
             @pl.when(has_off)
             def _():
                 off_copy(ref, far, s, 0).start()
 
-        @pl.loop(0, blocks)
-        def _(k):
-            s = order(k)
-            for offset in range(1, pieces):
-                arrived(ref.at[blocks + s, part_rows(offset)], share_recv.at[offset - 1, s])
-                on_copy(ref, s, offset, part_rows(offset)).start()
-
-                @pl.when(has_off & jnp.logical_not(relayed(k, span)))
-                def _():
-                    off_copy(ref, far, s, offset).start()
+            if paired:
+                finish_block(which, ref, far, other_of, span, k)
+
+        if not paired:
+
+            @pl.loop(0, blocks)
+            def _(k):
+                finish_block(which, ref, far, other_of, span, k)
 
         for k in range(span[2]):
             relay(far, k, span)
+
+    def finish_block(which, ref, far, other_of, span, k):
+        s = order(k)
+        if paired:
+            mine_copy(which, s).wait()
+            for start in starts:
+                value = other_of(s, start, other_sum(which, s, start))
+                ref[blocks + s, other_rows(start), :] = value.astype(BF16)
+        for offset in range(1, pieces):
+            if not paired:
+                arrived(ref.at[blocks + s, part_rows(offset)], share_recv.at[offset - 1, s])
+            on_copy(ref, s, offset, part_rows(offset)).start()
+
+            @pl.when(has_off & jnp.logical_not(relayed(k, span)))
+            def _():
+                off_copy(ref, far, s, offset).start()
 
     def settle(ref):
         @pl.loop(0, blocks)
@@ -460,9 +540,11 @@
         pairs = [(b1, sigma), (b1, r), (b1, q), (r, r), (r, q), (q, q), (b1, b1)]
         return tuple(t + fold(x * y) for t, (x, y) in zip(totals, pairs))
 
-    sum_start(0, lax.fori_loop(0, blocks, sums1, (zero,) * 7))
+    term_start(0, lax.fori_loop(0, blocks, sums1, (zero,) * 7))
+    give(0)
+    sector_start(0)
     sent(raw, far1, span0, True)
-    got = sum_finish(0)
+    got = sum_finish(0, devices)
     theta1 = got(0)
     first_gram = got(6)
     weight = got(1) - theta1 * got(2)
@@ -479,7 +561,17 @@
         corr = (sig1[s, here, :] - theta1 * b1) * divided(s, start)
         return (corr - weight * b1) * scale1
 
-    spread(ext2, far2, base2, corr1, relays[1])
+    def first_other(s, start):
+        return raw[blocks + s, other_rows(start), :].astype(F32) * scale
+
+    def other1(s, start, sigma):
+        b1 = first_other(s, start)
+        corr = (sigma - theta1 * b1) * inverse_of[s, other_rows(start), :]
+        value = (corr - weight * b1) * scale1
+        other2[s, pl.ds(start, step), :] = value
+        return value
+
+    spread(0, ext2, far2, base2, corr1, other1, relays[1])
     settle(ext2)
     apply(ext2, far2, relays[1], False)
 
@@ -505,9 +597,11 @@
         ]
         return tuple(t + fold(x * y) for t, (x, y) in zip(totals, pairs))
 
-    sum_start(1, lax.fori_loop(0, blocks, sums2, (zero,) * 12))
+    term_start(1, lax.fori_loop(0, blocks, sums2, (zero,) * 12))
+    give(1)
+    sector_start(1)
     sent(ext2, far2, relays[1], False)
-    more = sum_finish(1)
+    more = sum_finish(1, devices)
     theta2 = more(0)
     weight1 = more(1) - theta2 * more(3)
     weight2 = more(2) - theta2 * more(4)
@@ -527,6 +621,12 @@
         corr = (sig2[s, here, :] - theta2 * b2) * divided(s, start)
         return (corr - weight1 * b1 - weight2 * b2) * scale2
 
+    def other2_of(s, start, sigma):
+        b1 = first_other(s, start)
+        b2 = other2[s, pl.ds(start, step), :]
+        corr = (sigma - theta2 * b2) * inverse_of[s, other_rows(start), :]
+        return (corr - weight1 * b1 - weight2 * b2) * scale2
+
     def cross(s, totals):
         for start in starts:
             here = pl.ds(start, step)
@@ -535,7 +635,7 @@
             totals = tuple(t + fold(x * y) for t, (x, y) in zip(totals, pairs))
         return totals
 
-    spread(ext3, far3, last, corr2, relays[2])
+    spread(1, ext3, far3, last, corr2, other2_of, relays[2])
     crossed = lax.fori_loop(0, blocks, cross, (zero,) * 2)
     settle(ext3)
 
@@ -563,7 +663,7 @@
             env[t, s] = (new * width ** (-0.5)).astype(BF16)
 
     sent(ext3, far3, relays[2], False)
-    end = sum_finish(2)
+    end = sum_finish(2, count)
     cells = [
         [theta1, more(10), end(0)],
         [more(11), theta2, end(1)],
@@ -577,8 +677,10 @@
             out = jnp.where((row == i) & (col == j), cells[i][j], out)
     proj[...] = out
 
-    for which in range(3):
-        arrived(slots.at[which, pl.ds(0, count - 1)], sum_send.at[which])
+    for which, members in enumerate((devices, devices, count)):
+        arrived(slots.at[which, pl.ds(0, members - 1)], sum_send.at[which])
+    for which in range(2):
+        arrived(term_slots.at[which, pl.ds(0, pieces - 1)], term_send.at[which])
     for i, (stride, radix) in enumerate(rounds):
         arrived(norm_slots.at[i, pl.ds(0, radix - 1)], norm_send.at[i])
 
@@ -614,7 +716,7 @@
     )(proj, last, env)
 
 
-RELAYS = ((0, 4, 2), (7, 8, 4), (4, 8, 4))
+RELAYS = ((0, 4, 4), (0, 2, 2), (0, 5, 3))
 
 
 def on_device(psi, left, right, connect, sector_dims, precond):
@@ -650,7 +752,7 @@
             pltpu.VMEM((terms, blocks, width, width), BF16),
             pltpu.VMEM((blocks, width, width), BF16),
             pltpu.VMEM((blocks, width, width), BF16),
-            pltpu.VMEM((blocks, share, width), F32),
+            pltpu.VMEM((blocks, width, width), F32),
             pltpu.VMEM((3 * blocks, width, width), BF16),
             pltpu.VMEM((blocks, width, width), BF16),
             pltpu.VMEM((blocks, width, width), BF16),
@@ -661,12 +763,17 @@
             pltpu.VMEM((blocks, width, width), F32),
             pltpu.VMEM((others, blocks, share, width), BF16),
             pltpu.VMEM((others, blocks, share, width), BF16),
+            pltpu.VMEM((blocks, share, width), BF16),
+            pltpu.VMEM((2, blocks, share, width), BF16),
+            pltpu.VMEM((blocks, share, width), F32),
             pltpu.VMEM((blocks, share, width), F32),
             pltpu.VMEM((blocks, share, width), F32),
             pltpu.VMEM((blocks, share, width), F32),
             pltpu.VMEM((blocks, share, width), F32),
             pltpu.VMEM((3, 1, 128), F32),
             pltpu.VMEM((3, count, 1, 128), F32),
+            pltpu.VMEM((2, 1, 128), F32),
+            pltpu.VMEM((2, pieces, 1, 128), F32),
             pltpu.VMEM((rounds, 1, 128), F32),
             pltpu.VMEM((rounds, 4, 1, 128), F32),
             dma((pieces, blocks)),
@@ -676,10 +783,14 @@
             dma((others, blocks)),
             dma((others, blocks)),
             dma((others, blocks)),
+            dma((2, blocks)),
+            dma((2, blocks)),
             dma((others, blocks)),
             dma((others, blocks)),
             dma((3,)),
             dma((3,)),
+            dma((2,)),
+            dma((2,)),
             dma((rounds,)),
             dma((rounds,)),
             dma((4,)),

time: 105 us -> 100 us (0.952)
  Pallas kernels: 104 us -> 99.5 us
    pallas_call x1, Pallas kernels: 101 us -> 96.9 us  [on_device(): pl.pallas_call(functools.partial(kernel, sizes, RELAYS), name='davidson',...]
where the time goes in v2:
time: 100 us
  Pallas kernels  99.5 us (100%)
    pallas_call x1, Pallas kernels, on_device(): pl.pallas_call(functools.partial(kernel, sizes, RELAYS), name='davidson',...  96.9 us
    pallas_call x1, Pallas kernels, write(): pl.pallas_call(write_kernel, name='write', out_shape=(jax.ShapeDtypeStruc...  2.61 us

profile of v2, /device:TPU:0, one launch (start us, length us, event | category | flops | bytes accessed | tf_op | source)
XLA Modules:
  0.0 100.2 jit_solution(14386762095608343502)
XLA Ops:
  0.6 96.9 %davidson.1 = (f32[8,128]{1,0:T(8,128)S(1)}, f32[8,128,256]{2,1,0:T(8,128)S(1)}, bf16[3,8,256,256]{3,2,1,0:T(8,128)(2,1)S(1)}) custom-call(s32[2,8]{1,0:T(2,128)} %dims.1, s32[3,8]{1,0:T(4,128)} %conn.1, bf16[8,256,256]{2,1,0:T(8,128)(2,1)} %psi_in.1, bf16[3,8,256,256]{3,2,1,0:T(8,128)(2,1)} %left_in.1, bf16[3,8,256,256]{3,2,1,0:T(8,128)(2,1)} %right_in.1, ...), custom_call_target="tpu_custom_call" | custom-call | tf_op jit(solution)/shard_map/davidson/pallas_call | solution.py:740
  97.6 2.6 %write.1 = (f32[3,3]{1,0:T(4,128)}, f32[8,128,256]{2,1,0:T(8,128)}, bf16[3,8,256,256]{3,2,1,0:T(8,128)(2,1)}) custom-call(f32[8,128]{1,0:T(8,128)S(1)} %get-tuple-element.6.proj, f32[8,128,256]{2,1,0:T(8,128)S(1)} %get-tuple-element.7.last, bf16[3,8,256,256]{3,2,1,0:T(8,128)(2,1)S(1)} %get-tuple-element.8.env), custom_call_target="tpu_custom_call" | custom-call | tf_op jit(solution)/shard_map/write/pallas_call | solution.py:704

commit v3 on v2

--- a/solution.py
+++ b/solution.py
@@ -31,13 +31,13 @@
 
 
 def kernel(
-    sizes, relays,
+    sizes, relays, early,
     dims, conn, psi_in, left_in, right_in, pre_in,
     proj, last, env,
     left, right, pre, psi, inverse_of, raw, far1, far2, far3, ext1, ext2, ext3, acc, stage, came, mine, given, other2, sig1, sig2, base1, base2,
-    tile, slots, term_tile, term_slots, norm_tile, norm_slots,
+    pre_far, sig_out, sig_far, base_far, tile, slots, norm_tile, norm_slots,
     on_send, on_recv, off_send, off_recv, relay_send, share_send, share_recv, mine_send, mine_recv, part_send, part_recv,
-    sum_send, sum_recv, term_send, term_recv, norm_send, norm_recv, load,
+    pre_send, pre_recv, sig_send, sig_recv, sum_send, sum_recv, norm_send, norm_recv, load,
 ):
     pieces, devices, terms, blocks, width, entries = sizes
     share = width // pieces
@@ -146,6 +146,26 @@
     def off_arrived(far, s, j):
         arrived(far.at[s, part_rows(j)], off_recv.at[j, s])
 
+    def pre_copy(k):
+        return pltpu.make_async_remote_copy(
+            src_ref=pre.at[order(k)],
+            dst_ref=pre_far.at[k],
+            send_sem=pre_send.at[k],
+            recv_sem=pre_recv.at[k],
+            device_id=(me_t, off_s),
+            device_id_type=MESH,
+        )
+
+    def sig_copy(which, k, j):
+        return pltpu.make_async_remote_copy(
+            src_ref=sig_out.at[which, k, part_rows(j)],
+            dst_ref=sig_far.at[which, k, part_rows(j)],
+            send_sem=sig_send.at[which, j, k],
+            recv_sem=sig_recv.at[which, j, k],
+            device_id=(me_t, off_s),
+            device_id_type=MESH,
+        )
+
     def relay_copy(far, s, j):
         return pltpu.make_async_remote_copy(
             src_ref=far.at[s, rows_of(me_t)],
@@ -167,19 +187,21 @@
             for j in range(1, pieces):
                 relay_copy(far, s, j).start()
 
-    def receive(far, k, span):
+    def receive(far, k, span, low):
         s = turn(k)
 
-        @pl.when(has_off & jnp.logical_not(relayed(k, span)))
+        @pl.when(has_off & (k >= low) & jnp.logical_not(relayed(k, span)))
         def _():
             off_arrived(far, s, 0)
 
-        @pl.when(has_off)
+        @pl.when(has_off & (k >= low))
         def _():
             for j in range(1, pieces):
                 off_arrived(far, s, j)
 
-    def sent(ref, far, span, whole):
+    def sent(ref, far, span, low, which):
+        whole = which is None
+
         @pl.loop(0, blocks)
         def _(k):
             s = order(k)
@@ -192,11 +214,11 @@
                     for offset in range(1, pieces):
                         share_copy(ref, s, offset, me_t).wait_send()
 
-            @pl.when(has_off)
+            @pl.when(has_off & (k >= low))
             def _():
                 off_copy(ref, far, s, 0).wait_send()
 
-            @pl.when(has_off & jnp.logical_not(relayed(k, span)))
+            @pl.when(has_off & (k >= low) & jnp.logical_not(relayed(k, span)))
             def _():
                 for j in range(1, pieces):
                     off_copy(ref, far, s, j).wait_send()
@@ -205,6 +227,15 @@
             def _():
                 for j in range(1, pieces):
                     relay_copy(far, turn(k), j).wait_send()
+
+        @pl.when(has_off)
+        def _():
+            for k in range(early):
+                if whole:
+                    pre_copy(k).wait_send()
+                else:
+                    for j in range(pieces):
+                        sig_copy(which, k, j).wait_send()
 
     def share_copy(ref, s, offset, piece):
         return pltpu.make_async_remote_copy(
@@ -244,37 +275,6 @@
             row = jnp.sum(one, axis=0, keepdims=True)
             packed = jnp.where(lane == i, jnp.sum(row, axis=1, keepdims=True), packed)
         return packed
-
-    def term_start(which, tiles):
-        packed = pack(tiles)
-        term_tile[which] = packed
-        term_slots[which, me_t] = packed
-        for offset in range(1, pieces):
-            pltpu.make_async_remote_copy(
-                src_ref=term_tile.at[which],
-                dst_ref=term_slots.at[which, me_t],
-                send_sem=term_send.at[which],
-                recv_sem=term_recv.at[which],
-                device_id=(term_at(offset), me_s),
-                device_id_type=MESH,
-            ).start()
-
-    def sector_start(which):
-        arrived(term_slots.at[which, pl.ds(0, pieces - 1)], term_recv.at[which])
-        packed = jnp.sum(term_slots[which], axis=0)
-        tile[which] = packed
-        slots[which, me_s] = packed
-
-        @pl.loop(1, devices)
-        def _(offset):
-            pltpu.make_async_remote_copy(
-                src_ref=tile.at[which],
-                dst_ref=slots.at[which, me_s],
-                send_sem=sum_send.at[which],
-                recv_sem=sum_recv.at[which],
-                device_id=(me_t, lax.rem(me_s + offset, devices)),
-                device_id_type=MESH,
-            ).start()
 
     def sum_start(which, tiles):
         packed = pack(tiles)
@@ -292,10 +292,10 @@
                 device_id_type=MESH,
             ).start()
 
-    def sum_finish(which, members):
-        others = slots.at[which, pl.ds(0, members - 1)]
+    def sum_finish(which):
+        others = slots.at[which, pl.ds(0, count - 1)]
         arrived(others, sum_recv.at[which])
-        full = jnp.sum(slots[which, pl.ds(0, members)], axis=0) / entries
+        full = jnp.sum(slots[which], axis=0) / entries
         return lambda i: full[:, i : i + 1]
 
     def norm_start(i, packed):
@@ -362,6 +362,11 @@
         for start in strips:
             here = pl.ds(start, step)
             inverse_of[s, here, :] = 1.0 / pre[s, here, :].astype(F32)
+
+    @pl.when(has_off)
+    def _():
+        for k in range(early):
+            pre_copy(k).start()
 
     total = None
     for i in range(len(rounds)):
@@ -408,22 +413,38 @@
             total = one if total is None else total + one
         return total
 
-    def take(ref, far, k, span, scaling):
+    def take(ref, far, k, span, which, far_of):
         s = turn(k)
+        low = 0 if which is None else early
         relay(far, k + span[2], span)
-        receive(far, k, span)
-
-        @pl.when(has_off)
+        receive(far, k, span, low)
+
+        @pl.when(has_off & (k >= low))
         def _():
-            if scaling:
+            if which is None:
                 scaled(far, s, off_slot(s))
             else:
                 ref[off_slot(s)] = far[s]
 
-    def apply(ref, far, span, scaling):
+        if low:
+
+            @pl.when(has_off & (k < low))
+            def _():
+                if which == 0:
+                    arrived(pre_far.at[k], pre_recv.at[k])
+                for j in range(pieces):
+                    arrived(sig_far.at[which, k, part_rows(j)], sig_recv.at[which, j, k])
+                for start in strips:
+                    here = pl.ds(start, step)
+                    b1 = far1[s, here, :].astype(F32) * scale
+                    sigma = sig_far[which, k, here, :].astype(F32)
+                    inverse = 1.0 / pre_far[k, here, :].astype(F32)
+                    ref[off_slot(s), here, :] = far_of(k, here, sigma, b1, inverse).astype(BF16)
+
+    def apply(ref, far, span, which, far_of):
         @pl.loop(0, blocks)
         def _(k):
-            take(ref, far, k, span, scaling)
+            take(ref, far, k, span, which, far_of)
             s = turn(k)
             acc[s] = product(ref, s, False)
             for offset in range(1, pieces):
@@ -452,11 +473,32 @@
         if not paired:
             return
 
+        for k in range(early):
+            s = order(k)
+            for start in starts:
+                sigma = (sig1, sig2)[which][s, pl.ds(start, step), :]
+                sig_out[which, k, own_rows(start), :] = sigma.astype(BF16)
+
+            @pl.when(has_off)
+            def _():
+                sig_copy(which, k, 0).start()
+
         @pl.loop(0, blocks)
         def _(k):
             s = order(k)
             mine[s] = acc[s, rows_of(me_t), :].astype(BF16)
             mine_copy(which, s).start()
+
+        for k in range(early):
+            s = order(k)
+            mine_copy(which, s).wait()
+            for start in starts:
+                sigma = other_sum(which, s, start)
+                sig_out[which, k, other_rows(start), :] = sigma.astype(BF16)
+
+            @pl.when(has_off)
+            def _():
+                sig_copy(which, k, 1).start()
 
     def divided(s, start):
         return inverse_of[s, own_rows(start), :]
@@ -479,7 +521,7 @@
                     share_copy(ref, s, offset, me_t).start()
             on_copy(ref, s, 0, part_rows(0)).start()
 
-            @pl.when(has_off)
+            @pl.when(has_off & (k >= early))
             def _():
                 off_copy(ref, far, s, 0).start()
 
@@ -498,7 +540,10 @@
     def finish_block(which, ref, far, other_of, span, k):
         s = order(k)
         if paired:
-            mine_copy(which, s).wait()
+            @pl.when(k >= early)
+            def _():
+                mine_copy(which, s).wait()
+
             for start in starts:
                 value = other_of(s, start, other_sum(which, s, start))
                 ref[blocks + s, other_rows(start), :] = value.astype(BF16)
@@ -507,7 +552,7 @@
                 arrived(ref.at[blocks + s, part_rows(offset)], share_recv.at[offset - 1, s])
             on_copy(ref, s, offset, part_rows(offset)).start()
 
-            @pl.when(has_off & jnp.logical_not(relayed(k, span)))
+            @pl.when(has_off & (k >= early) & jnp.logical_not(relayed(k, span)))
             def _():
                 off_copy(ref, far, s, offset).start()
 
@@ -520,7 +565,7 @@
 
     loads[2].wait()
     loads[3].wait()
-    apply(ext1, far1, span0, True)
+    apply(ext1, far1, span0, None, None)
 
     def sums1(k, totals):
         s = turn(k)
@@ -540,11 +585,10 @@
         pairs = [(b1, sigma), (b1, r), (b1, q), (r, r), (r, q), (q, q), (b1, b1)]
         return tuple(t + fold(x * y) for t, (x, y) in zip(totals, pairs))
 
-    term_start(0, lax.fori_loop(0, blocks, sums1, (zero,) * 7))
+    sum_start(0, lax.fori_loop(0, blocks, sums1, (zero,) * 7))
     give(0)
-    sector_start(0)
-    sent(raw, far1, span0, True)
-    got = sum_finish(0, devices)
+    sent(raw, far1, span0, 0, None)
+    got = sum_finish(0)
     theta1 = got(0)
     first_gram = got(6)
     weight = got(1) - theta1 * got(2)
@@ -573,7 +617,16 @@
 
     spread(0, ext2, far2, base2, corr1, other1, relays[1])
     settle(ext2)
-    apply(ext2, far2, relays[1], False)
+    def far1_of(k, here, sigma, b1, inverse):
+        value = ((sigma - theta1 * b1) * inverse - weight * b1) * scale1
+        base_far[k, here, :] = value
+        return value
+
+    def far2_of(k, here, sigma, b1, inverse):
+        b2 = base_far[k, here, :]
+        return ((sigma - theta2 * b2) * inverse - weight1 * b1 - weight2 * b2) * scale2
+
+    apply(ext2, far2, relays[1], 0, far1_of)
 
     def sums2(k, totals):
         s = turn(k)
@@ -597,11 +650,10 @@
         ]
         return tuple(t + fold(x * y) for t, (x, y) in zip(totals, pairs))
 
-    term_start(1, lax.fori_loop(0, blocks, sums2, (zero,) * 12))
+    sum_start(1, lax.fori_loop(0, blocks, sums2, (zero,) * 12))
     give(1)
-    sector_start(1)
-    sent(ext2, far2, relays[1], False)
-    more = sum_finish(1, devices)
+    sent(ext2, far2, relays[1], early, 0)
+    more = sum_finish(1)
     theta2 = more(0)
     weight1 = more(1) - theta2 * more(3)
     weight2 = more(2) - theta2 * more(4)
@@ -640,7 +692,7 @@
     settle(ext3)
 
     def sums3(k, totals):
-        take(ext3, far3, k, relays[2], False)
+        take(ext3, far3, k, relays[2], 1, far2_of)
         s = turn(k)
         acc[s] = product(ext3, s, True)
 
@@ -662,8 +714,8 @@
             )
             env[t, s] = (new * width ** (-0.5)).astype(BF16)
 
-    sent(ext3, far3, relays[2], False)
-    end = sum_finish(2, count)
+    sent(ext3, far3, relays[2], early, 1)
+    end = sum_finish(2)
     cells = [
         [theta1, more(10), end(0)],
         [more(11), theta2, end(1)],
@@ -677,10 +729,8 @@
             out = jnp.where((row == i) & (col == j), cells[i][j], out)
     proj[...] = out
 
-    for which, members in enumerate((devices, devices, count)):
-        arrived(slots.at[which, pl.ds(0, members - 1)], sum_send.at[which])
-    for which in range(2):
-        arrived(term_slots.at[which, pl.ds(0, pieces - 1)], term_send.at[which])
+    for which in range(3):
+        arrived(slots.at[which, pl.ds(0, count - 1)], sum_send.at[which])
     for i, (stride, radix) in enumerate(rounds):
         arrived(norm_slots.at[i, pl.ds(0, radix - 1)], norm_send.at[i])
 
@@ -716,7 +766,8 @@
     )(proj, last, env)
 
 
-RELAYS = ((0, 4, 4), (0, 2, 2), (0, 5, 3))
+EARLY = 2
+RELAYS = ((0, 4, 4), (0, 0, 0), (2, 6, 5))
 
 
 def on_device(psi, left, right, connect, sector_dims, precond):
@@ -729,6 +780,8 @@
     sizes = (pieces, devices, terms, blocks, width, entries)
     others = max(pieces - 1, 1)
     rounds = len(rounds_of(devices))
+    early = min(EARLY, blocks) if pieces == 2 else 0
+    ahead = max(early, 1)
     dma = pltpu.SemaphoreType.DMA
     vmem = pl.BlockSpec(memory_space=pltpu.VMEM)
     smem = pl.BlockSpec(memory_space=pltpu.SMEM)
@@ -738,7 +791,7 @@
         for one in (sector_dims, connect, psi, left, right, precond)
     ]
     proj, last, env = pl.pallas_call(
-        functools.partial(kernel, sizes, RELAYS),
+        functools.partial(kernel, sizes, RELAYS, early),
         name="davidson",
         out_shape=(
             jax.ShapeDtypeStruct((8, 128), F32),
@@ -770,10 +823,12 @@
             pltpu.VMEM((blocks, share, width), F32),
             pltpu.VMEM((blocks, share, width), F32),
             pltpu.VMEM((blocks, share, width), F32),
+            pltpu.VMEM((ahead, width, width), BF16),
+            pltpu.VMEM((2, ahead, width, width), BF16),
+            pltpu.VMEM((2, ahead, width, width), BF16),
+            pltpu.VMEM((ahead, width, width), F32),
             pltpu.VMEM((3, 1, 128), F32),
             pltpu.VMEM((3, count, 1, 128), F32),
-            pltpu.VMEM((2, 1, 128), F32),
-            pltpu.VMEM((2, pieces, 1, 128), F32),
             pltpu.VMEM((rounds, 1, 128), F32),
             pltpu.VMEM((rounds, 4, 1, 128), F32),
             dma((pieces, blocks)),
@@ -787,10 +842,12 @@
             dma((2, blocks)),
             dma((others, blocks)),
             dma((others, blocks)),
+            dma((ahead,)),
+            dma((ahead,)),
+            dma((2, pieces, ahead)),
+            dma((2, pieces, ahead)),
             dma((3,)),
             dma((3,)),
-            dma((2,)),
-            dma((2,)),
             dma((rounds,)),
             dma((rounds,)),
             dma((4,)),

time: 100 us -> 96.8 us (0.968)
  Pallas kernels: 99.5 us -> 96 us
    pallas_call x1, Pallas kernels: 96.9 us -> 93.4 us  [on_device(): pl.pallas_call(functools.partial(kernel, sizes, RELAYS, early), name='dav...]
where the time goes in v3:
time: 96.8 us; the launch traced here: 96.6 us
  Pallas kernels  96 us (99%)
    pallas_call x1, Pallas kernels, on_device(): pl.pallas_call(functools.partial(kernel, sizes, RELAYS, early), name='dav...  93.4 us
    pallas_call x1, Pallas kernels, write(): pl.pallas_call(write_kernel, name='write', out_shape=(jax.ShapeDtypeStruc...  2.61 us

profile of v3, /device:TPU:0, one launch (start us, length us, event | category | flops | bytes accessed | tf_op | source)
XLA Modules:
  0.0 96.6 jit_solution(4967290874933483885)
XLA Ops:
  0.6 93.4 %davidson.1 = (f32[8,128]{1,0:T(8,128)S(1)}, f32[8,128,256]{2,1,0:T(8,128)S(1)}, bf16[3,8,256,256]{3,2,1,0:T(8,128)(2,1)S(1)}) custom-call(s32[2,8]{1,0:T(2,128)} %dims.1, s32[3,8]{1,0:T(4,128)} %conn.1, bf16[8,256,256]{2,1,0:T(8,128)(2,1)} %psi_in.1, bf16[3,8,256,256]{3,2,1,0:T(8,128)(2,1)} %left_in.1, bf16[3,8,256,256]{3,2,1,0:T(8,128)(2,1)} %right_in.1, ...), custom_call_target="tpu_custom_call" | custom-call | tf_op jit(solution)/shard_map/davidson/pallas_call | solution.py:793
  94.0 2.6 %write.1 = (f32[3,3]{1,0:T(4,128)}, f32[8,128,256]{2,1,0:T(8,128)}, bf16[3,8,256,256]{3,2,1,0:T(8,128)(2,1)}) custom-call(f32[8,128]{1,0:T(8,128)S(1)} %get-tuple-element.6.proj, f32[8,128,256]{2,1,0:T(8,128)S(1)} %get-tuple-element.7.last, bf16[3,8,256,256]{3,2,1,0:T(8,128)(2,1)S(1)} %get-tuple-element.8.env), custom_call_target="tpu_custom_call" | custom-call | tf_op jit(solution)/shard_map/write/pallas_call | solution.py:754

commit v4 on v3

--- a/solution.py
+++ b/solution.py
@@ -341,39 +341,48 @@
     pl.semaphore_wait(barrier, greeted + apart.astype(jnp.int32))
     norm_start(0, own_norm)
 
+    def first_off(low, high):
+        @pl.loop(low, high)
+        def _(k):
+            s = order(k)
+
+            @pl.when(has_off)
+            def _():
+                off_copy(raw, far1, s, 0).start()
+
+            @pl.when(has_off & jnp.logical_not(relayed(k, span0)))
+            def _():
+                for j in range(1, pieces):
+                    off_copy(raw, far1, s, j).start()
+
+    first_off(0, HEAD)
+
     @pl.loop(0, blocks)
     def _(k):
-        s = order(k)
-        on_copy(raw, s, 0, everything).start()
+        on_copy(raw, order(k), 0, everything).start()
+
+    def finish_loads():
+        loads[1].wait()
+
+        @pl.loop(0, blocks)
+        def _(s):
+            for start in strips:
+                here = pl.ds(start, step)
+                inverse_of[s, here, :] = 1.0 / pre[s, here, :].astype(F32)
 
         @pl.when(has_off)
         def _():
-            off_copy(raw, far1, s, 0).start()
-
-        @pl.when(has_off & jnp.logical_not(relayed(k, span0)))
-        def _():
-            for j in range(1, pieces):
-                off_copy(raw, far1, s, j).start()
-
-    loads[1].wait()
-
-    @pl.loop(0, blocks)
-    def _(s):
-        for start in strips:
-            here = pl.ds(start, step)
-            inverse_of[s, here, :] = 1.0 / pre[s, here, :].astype(F32)
-
-    @pl.when(has_off)
-    def _():
-        for k in range(early):
-            pre_copy(k).start()
+            for k in range(early):
+                pre_copy(k).start()
 
     total = None
     for i in range(len(rounds)):
         total = norm_finish(i)
         if i + 1 < len(rounds):
             norm_start(i + 1, total)
-        if i == 0:
+        if i == max(len(rounds) - 2, 0):
+            first_off(HEAD, blocks)
+            finish_loads()
             for k in range(relays[0][2]):
                 relay(far1, k, span0)
     norm = total[:, 0:1] / entries
@@ -766,8 +775,9 @@
     )(proj, last, env)
 
 
-EARLY = 2
-RELAYS = ((0, 4, 4), (0, 0, 0), (2, 6, 5))
+HEAD = 3
+EARLY = 3
+RELAYS = ((0, 4, 4), (0, 0, 0), (3, 6, 6))
 
 
 def on_device(psi, left, right, connect, sector_dims, precond):

time: 96.8 us -> 92.9 us (0.960)
  Pallas kernels: 96 us -> 92.1 us
    pallas_call x1, Pallas kernels: 93.4 us -> 89.5 us  [on_device(): pl.pallas_call(functools.partial(kernel, sizes, RELAYS, early), name='dav...]
where the time goes in v4:
time: 92.9 us; the launch traced here: 92.8 us
  Pallas kernels  92.1 us (99%)
    pallas_call x1, Pallas kernels, on_device(): pl.pallas_call(functools.partial(kernel, sizes, RELAYS, early), name='dav...  89.5 us
    pallas_call x1, Pallas kernels, write(): pl.pallas_call(write_kernel, name='write', out_shape=(jax.ShapeDtypeStruc...  2.61 us

profile of v4, /device:TPU:0, one launch (start us, length us, event | category | flops | bytes accessed | tf_op | source)
XLA Modules:
  0.0 92.8 jit_solution(5748092395616186660)
XLA Ops:
  0.6 89.5 %davidson.1 = (f32[8,128]{1,0:T(8,128)S(1)}, f32[8,128,256]{2,1,0:T(8,128)S(1)}, bf16[3,8,256,256]{3,2,1,0:T(8,128)(2,1)S(1)}) custom-call(s32[2,8]{1,0:T(2,128)} %dims.1, s32[3,8]{1,0:T(4,128)} %conn.1, bf16[8,256,256]{2,1,0:T(8,128)(2,1)} %psi_in.1, bf16[3,8,256,256]{3,2,1,0:T(8,128)(2,1)} %left_in.1, bf16[3,8,256,256]{3,2,1,0:T(8,128)(2,1)} %right_in.1, ...), custom_call_target="tpu_custom_call" | custom-call | tf_op jit(solution)/shard_map/davidson/pallas_call | solution.py:803
  90.2 2.6 %write.1 = (f32[3,3]{1,0:T(4,128)}, f32[8,128,256]{2,1,0:T(8,128)}, bf16[3,8,256,256]{3,2,1,0:T(8,128)(2,1)}) custom-call(f32[8,128]{1,0:T(8,128)S(1)} %get-tuple-element.6.proj, f32[8,128,256]{2,1,0:T(8,128)S(1)} %get-tuple-element.7.last, bf16[3,8,256,256]{3,2,1,0:T(8,128)(2,1)S(1)} %get-tuple-element.8.env), custom_call_target="tpu_custom_call" | custom-call | tf_op jit(solution)/shard_map/write/pallas_call | solution.py:763

commit v5 on v4

--- a/solution.py
+++ b/solution.py
@@ -478,6 +478,16 @@
         total = acc[s, other_rows(start), :] + given[which, s, pl.ds(start, step), :].astype(F32)
         return masked(s, term_at(1) * share + start, total)
 
+    def give_blocks(which, low, high):
+        if not paired:
+            return
+
+        @pl.loop(low, high)
+        def _(k):
+            s = order(k)
+            mine[s] = acc[s, rows_of(me_t), :].astype(BF16)
+            mine_copy(which, s).start()
+
     def give(which):
         if not paired:
             return
@@ -492,11 +502,7 @@
             def _():
                 sig_copy(which, k, 0).start()
 
-        @pl.loop(0, blocks)
-        def _(k):
-            s = order(k)
-            mine[s] = acc[s, rows_of(me_t), :].astype(BF16)
-            mine_copy(which, s).start()
+        give_blocks(which, FIRST, blocks)
 
         for k in range(early):
             s = order(k)
@@ -594,6 +600,7 @@
         pairs = [(b1, sigma), (b1, r), (b1, q), (r, r), (r, q), (q, q), (b1, b1)]
         return tuple(t + fold(x * y) for t, (x, y) in zip(totals, pairs))
 
+    give_blocks(0, 0, FIRST)
     sum_start(0, lax.fori_loop(0, blocks, sums1, (zero,) * 7))
     give(0)
     sent(raw, far1, span0, 0, None)
@@ -659,6 +666,7 @@
         ]
         return tuple(t + fold(x * y) for t, (x, y) in zip(totals, pairs))
 
+    give_blocks(1, 0, FIRST)
     sum_start(1, lax.fori_loop(0, blocks, sums2, (zero,) * 12))
     give(1)
     sent(ext2, far2, relays[1], early, 0)
@@ -776,8 +784,9 @@
 
 
 HEAD = 3
+FIRST = 2
 EARLY = 3
-RELAYS = ((0, 4, 4), (0, 0, 0), (3, 6, 6))
+RELAYS = ((0, 4, 4), (0, 0, 0), (3, 7, 6))
 
 
 def on_device(psi, left, right, connect, sector_dims, precond):

time: 92.9 us -> 90.1 us (0.970)
  Pallas kernels: 92.1 us -> 89.3 us
    pallas_call x1, Pallas kernels: 89.5 us -> 86.7 us  [on_device(): pl.pallas_call(functools.partial(kernel, sizes, RELAYS, early), name='dav...]
where the time goes in v5:
time: 90.1 us; the launch traced here: 89.9 us
  Pallas kernels  89.3 us (99%)
    pallas_call x1, Pallas kernels, on_device(): pl.pallas_call(functools.partial(kernel, sizes, RELAYS, early), name='dav...  86.7 us
    pallas_call x1, Pallas kernels, write(): pl.pallas_call(write_kernel, name='write', out_shape=(jax.ShapeDtypeStruc...  2.61 us

profile of v5, /device:TPU:0, one launch (start us, length us, event | category | flops | bytes accessed | tf_op | source)
XLA Modules:
  0.0 89.9 jit_solution(1478018288926854476)
XLA Ops:
  0.6 86.7 %davidson.1 = (f32[8,128]{1,0:T(8,128)S(1)}, f32[8,128,256]{2,1,0:T(8,128)S(1)}, bf16[3,8,256,256]{3,2,1,0:T(8,128)(2,1)S(1)}) custom-call(s32[2,8]{1,0:T(2,128)} %dims.1, s32[3,8]{1,0:T(4,128)} %conn.1, bf16[8,256,256]{2,1,0:T(8,128)(2,1)} %psi_in.1, bf16[3,8,256,256]{3,2,1,0:T(8,128)(2,1)} %left_in.1, bf16[3,8,256,256]{3,2,1,0:T(8,128)(2,1)} %right_in.1, ...), custom_call_target="tpu_custom_call" | custom-call | tf_op jit(solution)/shard_map/davidson/pallas_call | solution.py:812
  87.3 2.6 %write.1 = (f32[3,3]{1,0:T(4,128)}, f32[8,128,256]{2,1,0:T(8,128)}, bf16[3,8,256,256]{3,2,1,0:T(8,128)(2,1)}) custom-call(f32[8,128]{1,0:T(8,128)S(1)} %get-tuple-element.6.proj, f32[8,128,256]{2,1,0:T(8,128)S(1)} %get-tuple-element.7.last, bf16[3,8,256,256]{3,2,1,0:T(8,128)(2,1)S(1)} %get-tuple-element.8.env), custom_call_target="tpu_custom_call" | custom-call | tf_op jit(solution)/shard_map/write/pallas_call | solution.py:771
